TPU v7x, 32 devices: a whole 2x2x4 slice. The times are simulated.
32 devices in a mesh: dp: 4 (over z), feat: 8 (over y, x, core).
Axes of the slice: x: 2, y: 2, z: 4, core: 2. Of those that a mesh axis runs over, the one named last changes fastest.
Arguments:
- clip_feats: bfloat16 [2, 384, 8192], P(None, 'dp', 'feat'), may hold values from 0 to 60
- proj_weight: bfloat16 [8192, 8192], P('dp', 'feat'), may hold values from -0.0625 to 0.0625
Outputs:
- loss_value: float32 [], replicated
- weight_grad: float32 [8192, 8192], P('dp', 'feat')
- redundancy: float32 [], replicated
- pair_similarity: float32 [384, 384], P('dp')
All inputs are finite; a program needn't handle non-finite values.
Results may differ from a plain program's by a relative error of at most 0.034.
Values may be sent and summed in bfloat16 or wider, within the bound.
A program may use at most 64 MiB of HBM per device.

v0:
```python
import math

import jax
import jax.numpy as jnp
from jax import lax
from jax.sharding import PartitionSpec as P

D = 8192


off_weight = 0.0051
epsilon = 1e-05
grad_scale = 32.0


def per_device(clip_feats, proj_weight):
    pairs = clip_feats.shape[1]
    width = clip_feats.shape[2]
    dp_count = lax.axis_size("dp")
    pair_count = float(pairs * dp_count)
    gathered = lax.all_gather(clip_feats, "feat", axis=2, tiled=True)
    stacked = gathered.reshape(2 * pairs, gathered.shape[2])
    projected = jnp.dot(
        stacked,
        lax.all_gather(proj_weight, "dp", axis=0, tiled=True),
        preferred_element_type=jnp.float32,
    ).reshape(2, pairs, width)
    col_mean = lax.psum(jnp.sum(projected, axis=1), "dp")[:, None, :] / pair_count
    centered = projected - col_mean
    col_var = lax.psum(jnp.sum(centered * centered, axis=1), "dp")[:, None, :] / pair_count
    col_scale = lax.rsqrt(col_var + epsilon)
    normed = centered * col_scale
    quantized = normed.astype(jnp.bfloat16)
    widened = quantized.astype(jnp.float32)
    batch_all = lax.all_gather(quantized, "dp", axis=1, tiled=True)
    gram_part = jnp.einsum("vpc,vnc->vpn", quantized, batch_all, preferred_element_type=jnp.float32)
    grams = lax.psum(gram_part, "feat")
    total_pairs = grams.shape[2]
    row_ids = (
        lax.broadcasted_iota(jnp.int32, (pairs, total_pairs), 0) + lax.axis_index("dp") * pairs
    )
    col_ids = lax.broadcasted_iota(jnp.int32, (pairs, total_pairs), 1)
    pair_similarity = jnp.where(
        row_ids == col_ids, 0.0, (grams[0] + grams[1]) / (2.0 * math.sqrt(float(D)))
    )
    diag_corr = lax.psum(jnp.sum(widened[0] * widened[1], axis=0), "dp") / pair_count
    frobenius = jnp.sum(grams[0] * grams[1])
    diag_term = jnp.sum((1.0 - diag_corr) ** 2 - off_weight * diag_corr * diag_corr)
    dp_first = (lax.axis_index("dp") == 0).astype(jnp.float32)
    feat_first = (lax.axis_index("feat") == 0).astype(jnp.float32)
    frob_scaled = feat_first * frobenius / (pair_count * pair_count)
    loss_term = dp_first * diag_term + off_weight * frob_scaled
    off_term = frob_scaled - dp_first * jnp.sum(diag_corr * diag_corr)
    total_loss, off_sum = lax.psum((loss_term, off_term), ("dp", "feat"))
    loss_value = 16.0 * total_loss / float(D)
    redundancy = 8.0 * pair_count * off_sum / (float(D) * float(D))
    slope = -2.0 * (1.0 - diag_corr) - 2.0 * off_weight * diag_corr
    coefficient = 2.0 * off_weight / (pair_count * pair_count)
    gram_q = grams.astype(jnp.bfloat16)
    cross_first = jnp.dot(gram_q[1], batch_all[0], preferred_element_type=jnp.float32)
    cross_second = jnp.dot(gram_q[0], batch_all[1], preferred_element_type=jnp.float32)
    grad_norm = jnp.stack(
        [
            slope * widened[1] / pair_count + coefficient * cross_first,
            slope * widened[0] / pair_count + coefficient * cross_second,
        ]
    )
    sum_one, sum_two = lax.psum(
        (jnp.sum(grad_norm, axis=1), jnp.sum(grad_norm * normed, axis=1)), "dp"
    )
    pre_grad = col_scale * (
        grad_norm - sum_one[:, None, :] / pair_count - normed * (sum_two[:, None, :] / pair_count)
    )
    pre_q = pre_grad.astype(jnp.bfloat16)
    flat_grad = pre_q.reshape(2 * pairs, width)
    summed = lax.psum_scatter(
        jnp.dot(stacked.T, flat_grad, preferred_element_type=jnp.float32).astype(jnp.bfloat16),
        "dp",
        scatter_dimension=0,
        tiled=True,
    ).astype(jnp.float32)
    return (loss_value, grad_scale * summed, redundancy, pair_similarity)


def solution(mesh):
    placed = (P(None, "dp", "feat"), P("dp", "feat"))
    return jax.shard_map(
        per_device,
        mesh=mesh,
        in_specs=placed,
        out_specs=(P(), P("dp", "feat"), P(), P("dp", None)),
        check_vma=False,
    )
```

profile of v0, /device:TPU:0, one launch (start us, length us, event | category | flops | bytes accessed | tf_op | source)
XLA Modules:
  0.0 791.4 jit_solution(3627898898711487195)
XLA Ops:
  7.2 0.7 all-gather.4.cloned.1.call-update
  7.9 0.0 all-gather.6.cloned.1.call-start
  7.9 0.7 all-gather.6.cloned.1.call-update
  8.6 0.0 all-gather.8.cloned.1.call-start
  8.7 36.3 %all-gather.4.cloned.1.call-done = bf16[2,96,8192]{2,1,0:T(8,128)(2,1)} async-done(((bf16[2,96,1024]{2,1,0:T(8,128)(2,1)}), bf16[2,96,8192]{2,1,0:T(8,128)(2,1)}) %all-gather.4.cloned.1.call-update) | async-done | bytes 3145744 | tf_op jit(solution)/shard_map/all_gather | solution.py:21
  45.0 288.4 %all-gather.6.cloned.1.call-done = bf16[8192,1024]{1,0:T(8,128)(2,1)} async-done(((bf16[2048,1024]{1,0:T(8,128)(2,1)}), bf16[8192,1024]{1,0:T(8,128)(2,1)}) %all-gather.6.cloned.1.call-update) | async-done | bytes 16777232 | tf_op jit(solution)/shard_map/all_gather | solution.py:25
  333.3 8.5 %fusion.16 = (f32[2,1024]{1,0:T(2,128)S(1)}, f32[2,96,1024]{2,1,0:T(8,128)S(1)}) fusion(bf16[2,96,8192]{2,1,0:T(8,128)(2,1)} %all-gather.4.cloned.1.call-done, bf16[8192,1024]{1,0:T(8,128)(2,1)} %all-gather.6.cloned.1.call-done), kind=kOutput, calls=%fused_computation.42 | convolution fusion | flops 3221420032 | bytes 20717568 | tf_op jit(solution)/shard_map/dot_general | solution.py:23
  341.8 8.8 %psum.56 = f32[2,1024]{1,0:T(2,128)S(1)} all-reduce(f32[2,1024]{1,0:T(2,128)S(1)} %get-tuple-element.19), channel_id=1, replica_groups=mesh['dp'=4,'feat'=8] {'dp'}, use_global_device_ids=true, to_apply=%region_1.0 | all-reduce | flops 2048 | bytes 16384 | tf_op jit(solution)/shard_map/psum | solution.py:28
  350.6 0.1 multiply_reduce_fusion.1
  350.7 10.3 %psum.57 = f32[2,1024]{1,0:T(2,128)S(1)} all-reduce(f32[2,1024]{1,0:T(2,128)S(1)} %multiply_reduce_fusion.1), channel_id=1, replica_groups=mesh['dp'=4,'feat'=8] {'dp'}, use_global_device_ids=true, to_apply=%region_3.0 | all-reduce | flops 2048 | bytes 16384 | tf_op jit(solution)/shard_map/psum | solution.py:30
  361.1 0.9 fusion.14
  362.0 0.0 all-reduce.4.cloned.1.call-start
  362.0 0.1 multiply_reduce_fusion.2
  362.1 8.7 %psum.58 = f32[1024]{0:T(1024)S(1)} all-reduce(f32[1024]{0:T(1024)S(1)} %multiply_reduce_fusion.2), channel_id=1, replica_groups=mesh['dp'=4,'feat'=8] {'dp'}, use_global_device_ids=true, to_apply=%region_5.6 | all-reduce | flops 1024 | bytes 8192 | tf_op jit(solution)/shard_map/psum | solution.py:46
  370.8 26.6 %all-gather.8.cloned.1.call-done = bf16[2,384,1024]{2,1,0:T(8,128)(2,1)} async-done(((bf16[2,96,1024]{2,1,0:T(8,128)(2,1)}), bf16[2,384,1024]{2,1,0:T(8,128)(2,1)}) %all-gather.8.cloned.1.call-update) | async-done | bytes 1572880 | tf_op jit(solution)/shard_map/all_gather | solution.py:35
  397.3 3.0 fusion.17
  400.3 0.0 reduce-scatter.2.cloned.1.call-start
  400.4 1.2 multiply_reduce_fusion.4
  401.6 50.8 %all-reduce.4.cloned.1.call-done = f32[2,96,384]{2,1,0:T(8,128)} async-done(((f32[2,96,384]{2,1,0:T(8,128)}), f32[2,96,384]{2,1,0:T(8,128)}) %all-reduce.4.cloned.1.call-update) | async-done | bytes 294928 | tf_op jit(solution)/shard_map/psum | solution.py:37
  452.4 1.0 convert_element_type.25
  453.4 1.4 fusion.4
  454.8 1.0 fusion.6
  455.8 0.7 copy-done.1
  456.6 0.2 fusion.8
  456.8 18.7 %all-reduce.1 = (f32[2,1024]{1,0:T(2,128)S(1)}, f32[2,1024]{1,0:T(2,128)S(1)}) all-reduce(f32[2,1024]{1,0:T(2,128)S(1)} %get-tuple-element.9, f32[2,1024]{1,0:T(2,128)S(1)} %get-tuple-element.8), channel_id=1, replica_groups=mesh['dp'=4,'feat'=8] {'dp'}, use_global_device_ids=true, to_apply=%region_13.14 | all-reduce | flops 4096 | bytes 32768 | tf_op jit(solution)/shard_map/psum | solution.py:68
  475.5 12.4 %fusion.2 = bf16[8192,1024]{0,1:T(8,128)(2,1)} fusion(bf16[2,96,8192]{2,1,0:T(8,128)(2,1)} %all-gather.4.cloned.1.call-done, f32[2,96,1024]{2,1,0:T(8,128)S(1)} %get-tuple-element.20, f32[1,96,1024]{2,1,0:T(8,128)S(1)} %fusion.4, f32[1,96,1024]{2,1,0:T(8,128)} %copy-done.1, f32[2,1024]{1,0:T(2,128)S(1)} %get-tuple-element.21, ...), kind=kOutput, calls=%fused_computation.3 | convolution fusion | flops 3231186944 | bytes 21528576 | tf_op jit(solution)/shard_map/dot_general | solution.py:77
  489.3 0.6 multiply_reduce_fusion.3
  490.6 41.4 %all-reduce = (f32[]{:T(128)}, f32[]{:T(128)}) all-reduce(f32[]{:T(128)S(6)} %add.47, f32[]{:T(128)S(6)} %sub.40), channel_id=1, replica_groups=mesh['dp'=4,'feat'=8] {'dp','feat'}, use_global_device_ids=true, to_apply=%region_9.10 | all-reduce | flops 2 | bytes 16 | tf_op jit(solution)/shard_map/psum | solution.py:54
  533.3 0.7 bitcast_select_fusion
  534.0 232.7 %reduce-scatter.2.cloned.1.call-done = bf16[2048,1024]{0,1:T(8,128)(2,1)} async-done(((bf16[8192,1024]{0,1:T(8,128)(2,1)}), bf16[2048,1024]{0,1:T(8,128)(2,1)}) %reduce-scatter.2.cloned.1.call-update) | async-done | bytes 4194320 | tf_op jit(solution)/shard_map/reduce_scatter | solution.py:76
  766.7 6.6 convert_multiply_fusion
  773.4 9.2 %copy.6 = f32[2048,1024]{1,0:T(8,128)} copy(f32[2048,1024]{0,1:T(8,128)} %convert_multiply_fusion) | data formatting | bytes 16777216
  (13 shorter events, 0.1 us)
Async XLA Ops:
  7.2 37.8 %all-gather.4.cloned.1.call-start = ((), (), s32[]{:S(2)}) async-start(), calls=%async_computation.1 | async-start | bytes 3538944 | tf_op jit(solution)/shard_map/all_gather | solution.py:21
  7.9 325.4 %all-gather.6.cloned.1.call-start = ((), (), s32[]{:S(2)}) async-start(), calls=%async_computation.2 | async-start | bytes 20971520 | tf_op jit(solution)/shard_map/all_gather | solution.py:25
  8.6 388.7 %all-gather.8.cloned.1.call-start = ((), (), s32[]{:S(2)}) async-start(), calls=%async_computation.3 | async-start | bytes 1966080 | tf_op jit(solution)/shard_map/all_gather | solution.py:35
  362.0 90.4 %all-reduce.4.cloned.1.call-start = ((), (), s32[]{:S(2)}) async-start(), calls=%async_computation.4 | async-start | bytes 589824 | tf_op jit(solution)/shard_map/psum | solution.py:37
  397.3 57.5 %copy-start = (bf16[2,384,1024]{2,1,0:T(8,128)(2,1)S(1)}, bf16[2,384,1024]{2,1,0:T(8,128)(2,1)}, u32[]{:S(2)}) copy-start(bf16[2,384,1024]{2,1,0:T(8,128)(2,1)} %all-gather.8.cloned.1.call-done) | copy-start | bytes 4718596
  400.3 366.4 %reduce-scatter.2.cloned.1.call-start = ((), (), s32[]{:S(2)}) async-start(), calls=%async_computation.5 | async-start | bytes 20971520 | tf_op jit(solution)/shard_map/reduce_scatter | solution.py:76
  455.8 0.7 copy-start.1
  487.9 1.4 copy-start.2
Sparse Core Ops, SparseCore 0:
  9.9 35.0 all-gather.3
  46.5 286.7 all-gather.5
  362.1 35.1 all-gather.7
  400.5 51.9 all-reduce.3
  488.0 278.6 reduce-scatter.1
where the time goes:
time: 792 us; the launch traced here: 791 us
  waiting for transfers between devices  636 us (80%)
  blocking collectives  87.9 us (11%)
  matrix products  26.2 us (3%)
  between operations  19.5 us (2%)
  other arithmetic  11.4 us (1%)
  local copies, waits for them, and re-layouts  9.99 us (1%)
    all_gather x1, waiting for transfers between devices, per_device(): lax.all_gather(proj_weight, 'dp', axis=0, tiled=True)  288 us
    reduce_scatter x1, waiting for transfers between devices, per_device(): lax.psum_scatter(jnp.dot(stacked.T, flat_grad, preferred_element_type=jnp...  233 us
    psum x1, waiting for transfers between devices, per_device(): grams = lax.psum(gram_part, 'feat')  50.8 us
    psum x1, blocking collectives, per_device(): total_loss, off_sum = lax.psum((loss_term, off_term), ('dp', 'feat'))  41.4 us
    all_gather x1, waiting for transfers between devices, per_device(): gathered = lax.all_gather(clip_feats, 'feat', axis=2, tiled=True)  36.3 us
    all_gather x1, waiting for transfers between devices, per_device(): batch_all = lax.all_gather(quantized, 'dp', axis=1, tiled=True)  26.6 us
    psum x1, blocking collectives, per_device(): lax.psum((jnp.sum(grad_norm, axis=1), jnp.sum(grad_norm * normed, axis=1)...  18.7 us
  transfers between devices with their start and end apart: 5, of which 5 were waited for; matrix products, arithmetic and copies ran while one was open for 0% of the time, Pallas kernels for 0%

commit v1 on v0

v1 whole, which is shorter than its diff:
```python
import math

import jax
import jax.numpy as jnp
from jax import lax
from jax.sharding import PartitionSpec as P

D = 8192


off_weight = 0.0051
epsilon = 1e-05
grad_scale = 32.0


def per_device(clip_feats, proj_weight):
    pairs = clip_feats.shape[1]
    width = clip_feats.shape[2]
    depth = proj_weight.shape[0]
    dp_count = lax.axis_size("dp")
    total = pairs * dp_count
    pair_count = float(total)
    gathered = lax.all_gather(clip_feats, "feat", axis=0, tiled=False)
    rows = lax.all_to_all(gathered, "dp", split_axis=0, concat_axis=0, tiled=True)
    parts = depth // width
    rows = rows.reshape(dp_count, parts, 2 * pairs, width).transpose(1, 0, 2, 3)
    rows = rows.reshape(parts, 2 * total, width)
    partial = sum(
        jnp.dot(rows[i], proj_weight[i * width : (i + 1) * width], preferred_element_type=jnp.float32)
        for i in range(parts)
    ).reshape(dp_count, 2, pairs, width)
    partial = partial - jnp.mean(partial, axis=(0, 2), keepdims=True)
    columns = width // dp_count
    pieces = partial.astype(jnp.bfloat16).reshape(2 * total, width)
    pieces = jnp.stack([pieces[:, i * columns : (i + 1) * columns] for i in range(dp_count)])
    pieces = lax.all_to_all(pieces, "dp", split_axis=0, concat_axis=0, tiled=True)
    centered = jnp.sum(pieces.astype(jnp.float32), axis=0)
    centered = centered.reshape(dp_count, 2, pairs, columns).transpose(1, 0, 2, 3).reshape(2, total, columns)
    col_var = jnp.mean(centered * centered, axis=1, keepdims=True)
    col_scale = lax.rsqrt(col_var + epsilon)
    normed = centered * col_scale
    quantized = normed.astype(jnp.bfloat16)
    widened = quantized.astype(jnp.float32)
    gram_part = jnp.einsum("vpc,vnc->vpn", quantized, quantized, preferred_element_type=jnp.float32)
    diag_corr = jnp.sum(widened[0] * widened[1], axis=0) / pair_count
    diag_part = jnp.sum((1.0 - diag_corr) ** 2 - off_weight * diag_corr * diag_corr)
    square_part = jnp.sum(diag_corr * diag_corr)
    grams, diag_term, squares = lax.psum((gram_part, diag_part, square_part), ("dp", "feat"))
    frob_scaled = jnp.sum(grams[0] * grams[1]) / (pair_count * pair_count)
    loss_value = 16.0 * (diag_term + off_weight * frob_scaled) / float(D)
    redundancy = 8.0 * pair_count * (frob_scaled - squares) / (float(D) * float(D))
    first_row = lax.axis_index("dp") * pairs
    own = lax.dynamic_slice_in_dim(grams, first_row, pairs, axis=1)
    row_ids = lax.broadcasted_iota(jnp.int32, (pairs, total), 0) + first_row
    col_ids = lax.broadcasted_iota(jnp.int32, (pairs, total), 1)
    pair_similarity = jnp.where(
        row_ids == col_ids, 0.0, (own[0] + own[1]) / (2.0 * math.sqrt(float(D)))
    )
    slope = -2.0 * (1.0 - diag_corr) - 2.0 * off_weight * diag_corr
    coefficient = 2.0 * off_weight / (pair_count * pair_count)
    gram_q = grams.astype(jnp.bfloat16)
    cross_first = jnp.dot(gram_q[1], quantized[0], preferred_element_type=jnp.float32)
    cross_second = jnp.dot(gram_q[0], quantized[1], preferred_element_type=jnp.float32)
    grad_norm = jnp.stack(
        [
            slope * widened[1] / pair_count + coefficient * cross_first,
            slope * widened[0] / pair_count + coefficient * cross_second,
        ]
    )
    mean_one = jnp.mean(grad_norm, axis=1, keepdims=True)
    mean_two = jnp.mean(grad_norm * normed, axis=1, keepdims=True)
    pre_q = (col_scale * (grad_norm - mean_one - normed * mean_two)).astype(jnp.bfloat16)
    pre_q = pre_q.reshape(2, dp_count, pairs, columns).transpose(1, 0, 2, 3).reshape(2 * total, columns)
    flat_grad = lax.all_gather(pre_q, "dp", axis=1, tiled=True)
    summed = jnp.concatenate(
        [jnp.dot(rows[i].T, flat_grad, preferred_element_type=jnp.float32) for i in range(parts)]
    )
    return (loss_value, grad_scale * summed, redundancy, pair_similarity)


def solution(mesh):
    placed = (P(None, "dp", "feat"), P("dp", "feat"))
    return jax.shard_map(
        per_device,
        mesh=mesh,
        in_specs=placed,
        out_specs=(P(), P("dp", "feat"), P(), P("dp", None)),
        check_vma=False,
    )
```

time: 792 us -> 369 us (0.47)
  waiting for transfers between devices: 636 us -> 166 us
  blocking collectives: 87.9 us -> 158 us
  matrix products: 26.2 us -> 10.8 us
    all_gather x3 -> x2, waiting for transfers between devices: 351 us -> 37 us  [the longest x1 37 us: per_device(): gathered = lax.all_gather(clip_feats, 'feat', axis=0, tiled=False)]
    reduce_scatter x1 -> x0, waiting for transfers between devices: 233 us -> none  [per_device(): lax.psum_scatter(jnp.dot(stacked.T, flat_grad, preferred_element_type=jnp...]
    all_to_all x0 -> x2, blocking collectives: none -> 115 us  [the longest x1 75.7 us: per_device(): lax.all_to_all(gathered, 'dp', split_axis=0, concat_axis=0, tiled=True)]
    psum x1, waiting for transfers between devices: 50.8 us -> 129 us  [per_device(): lax.psum((gram_part, diag_part, square_part), ('dp', 'feat'))]
    psum x5 -> x1, blocking collectives: 87.9 us -> 43.1 us  [per_device(): lax.psum((gram_part, diag_part, square_part), ('dp', 'feat'))]
    dot_general x5 -> x7, matrix products: 26.2 us -> 10.8 us  [the longest x2 5.24 us: per_device(): jnp.dot(rows[i].T, flat_grad, preferred_element_type=jnp.float32)]
  transfers between devices with their start and end apart: 5 -> 3, of which waited for: 5 -> 2; matrix products, arithmetic and copies ran while one was open for 0% -> 1% of each run, Pallas kernels for 0% -> 0%
where the time goes in v1:
time: 369 us; the launch traced here: 368 us
  waiting for transfers between devices  166 us (45%)
  blocking collectives  158 us (43%)
  between operations  18.8 us (5%)
  matrix products  10.8 us (3%)
  other arithmetic  10.2 us (3%)
    psum x1, waiting for transfers between devices, per_device(): lax.psum((gram_part, diag_part, square_part), ('dp', 'feat'))  129 us
    all_to_all x1, blocking collectives, per_device(): lax.all_to_all(gathered, 'dp', split_axis=0, concat_axis=0, tiled=True)  75.7 us
    psum x1, blocking collectives, per_device(): lax.psum((gram_part, diag_part, square_part), ('dp', 'feat'))  43.1 us
    all_to_all x1, blocking collectives, per_device(): lax.all_to_all(pieces, 'dp', split_axis=0, concat_axis=0, tiled=True)  39.1 us
    all_gather x1, waiting for transfers between devices, per_device(): gathered = lax.all_gather(clip_feats, 'feat', axis=0, tiled=False)  37 us
  transfers between devices with their start and end apart: 3, of which 2 were waited for; matrix products, arithmetic and copies ran while one was open for 1% of the time, Pallas kernels for 0%

profile of v1, /device:TPU:0, one launch (start us, length us, event | category | flops | bytes accessed | tf_op | source)
XLA Modules:
  0.0 367.6 jit_solution(855138404987530139)
XLA Ops:
  7.2 0.7 all-gather.6.cloned.1.call-update
  7.9 37.0 %all-gather.6.cloned.1.call-done = bf16[16,96,1024]{2,1,0:T(8,128)(2,1)} async-done(((bf16[2,96,1024]{2,1,0:T(8,128)(2,1)}), bf16[16,96,1024]{2,1,0:T(8,128)(2,1)}) %all-gather.6.cloned.1.call-update) | async-done | bytes 3145744 | tf_op jit(solution)/shard_map/all_gather | solution.py:23
  44.9 75.7 %all_to_all.10 = bf16[8,2,96,1024]{3,2,1,0:T(8,128)(2,1)S(1)} all-to-all(bf16[8,2,96,1024]{3,2,1,0:T(8,128)(2,1)} %bitcast.90), channel_id=1, replica_groups=mesh['dp'=4,'feat'=8] {'dp'}, dimensions={0} | all-to-all | bytes 6291456 | tf_op jit(solution)/shard_map/all_to_all | solution.py:24
  120.6 0.3 fusion.17
  121.0 3.0 copy-done.5
  123.9 1.8 fusion.1
  125.8 1.8 fusion.5
  127.6 0.2 reduce_sum.81
  127.8 0.4 fusion
  128.2 0.1 slice_bitcast_fusion.5
  128.3 0.2 pad_maximum_fusion
  128.5 39.1 %all_to_all.11 = bf16[4,768,256]{2,1,0:T(8,128)(2,1)S(1)} all-to-all(bf16[4,768,256]{2,1,0:T(8,128)(2,1)S(1)} %pad_maximum_fusion), channel_id=1, replica_groups=mesh['dp'=4,'feat'=8] {'dp'}, dimensions={0} | all-to-all | bytes 3145728 | tf_op jit(solution)/shard_map/all_to_all | solution.py:36
  167.7 0.2 convert_reduce_fusion
  167.9 0.1 multiply_reduce_fusion.1
  168.0 0.1 copy.9
  168.1 0.1 fusion.15
  168.2 1.4 fusion.18
  169.7 0.1 multiply_reduce_fusion.2
  169.7 0.6 multiply_reduce_fusion.3
  170.3 128.6 %all-reduce.3.cloned.1.call-done = f32[2,384,384]{2,1,0:T(8,128)} async-done(((f32[2,384,384]{2,1,0:T(8,128)}), f32[2,384,384]{2,1,0:T(8,128)}) %all-reduce.3.cloned.1.call-update) | async-done | bytes 1179664 | tf_op jit(solution)/shard_map/psum | solution.py:48
  298.9 1.3 convert_element_type.24
  300.3 0.3 fusion.9
  300.5 0.3 fusion.8
  300.8 0.1 maximum_reduce_fusion
  300.9 0.1 multiply_reduce_fusion
  301.0 0.9 multiply_convert_fusion
  302.0 43.1 %all-reduce = (f32[]{:T(128)}, f32[]{:T(128)}) all-reduce(f32[]{:T(128)} %get-tuple-element.5, f32[]{:T(128)} %get-tuple-element.4), channel_id=1, replica_groups=mesh['dp'=4,'feat'=8] {'dp','feat'}, use_global_device_ids=true, to_apply=%region_5.0 | all-reduce | flops 2 | bytes 16 | tf_op jit(solution)/shard_map/psum | solution.py:48
  345.0 0.8 fusion.11
  348.4 0.7 fusion.14
  349.2 3.4 convolution_bitcast_fusion
  352.6 1.8 convolution_bitcast_fusion.1
  354.4 4.4 %maximum_multiply_fusion = f32[2048,1024]{1,0:T(8,128)} fusion(f32[1024,1024]{1,0:T(8,128)S(1)} %convolution_bitcast_fusion, f32[1024,1024]{1,0:T(8,128)S(1)} %convolution_bitcast_fusion.1), kind=kLoop, calls=%fused_computation | loop fusion | flops 4194304 | bytes 16777216 | tf_op jit(solution)/shard_map/mul | solution.py:78
  (23 shorter events, 0.2 us)
Async XLA Ops:
  7.2 37.8 %all-gather.6.cloned.1.call-start = ((), (), s32[]{:S(2)}) async-start(), calls=%async_computation.4 | async-start | bytes 3538944 | tf_op jit(solution)/shard_map/all_gather | solution.py:23
  7.9 291.0 %all-reduce.3.cloned.1.call-start = ((), (), s32[]{:S(2)}) async-start(), calls=%async_computation.2 | async-start | bytes 2359296 | tf_op jit(solution)/shard_map/psum | solution.py:48
  120.6 3.3 copy-start.5
  120.9 4.8 %copy-start.3 = (bf16[1,4,192,1024]{3,2,0,1:T(8,128)(2,1)}, bf16[1,4,192,1024]{3,2,0,1:T(8,128)(2,1)S(1)}, u32[]{:S(2)}) copy-start(bf16[1,4,192,1024]{3,2,0,1:T(8,128)(2,1)S(1)} %get-tuple-element.11) | copy-start | bytes 4718596
  120.9 4.8 %copy-start.1 = (bf16[1,4,192,1024]{3,2,0,1:T(8,128)(2,1)}, bf16[1,4,192,1024]{3,2,0,1:T(8,128)(2,1)S(1)}, u32[]{:S(2)}) copy-start(bf16[1,4,192,1024]{3,2,0,1:T(8,128)(2,1)S(1)} %get-tuple-element.10) | copy-start | bytes 4718596
  169.6 179.5 %all-gather.4.cloned.1.call-start = ((), (), s32[]{:S(2)}) async-start(), calls=%async_computation.3 | async-start | bytes 1966080 | tf_op jit(solution)/shard_map/all_gather | solution.py:74
  301.0 44.0 %copy-start = (f32[2,384,384]{2,1,0:T(8,128)S(1)}, f32[2,384,384]{2,1,0:T(8,128)}, u32[]{:S(2)}) copy-start(f32[2,384,384]{2,1,0:T(8,128)} %all-reduce.3.cloned.1.call-done) | copy-start | bytes 3538948
  301.0 48.1 %copy-start.4 = (bf16[1,4,192,1024]{3,2,0,1:T(8,128)(2,1)S(1)}, bf16[1,4,192,1024]{3,2,0,1:T(8,128)(2,1)}, u32[]{:S(2)}) copy-start(bf16[1,4,192,1024]{3,2,0,1:T(8,128)(2,1)} %copy-done.3) | copy-start | bytes 4718596
  349.1 3.4 copy-start.2
  349.1 3.4 copy-start.6
Sparse Core Ops, SparseCore 0:
  9.9 35.0 all-gather.5
  169.7 129.1 all-reduce.2
  302.1 37.7 all-gather.3

commit v2 on v1

--- a/solution.py
+++ b/solution.py
@@ -1,8 +1,11 @@
+import functools
 import math
 
 import jax
 import jax.numpy as jnp
 from jax import lax
+from jax.experimental import pallas as pl
+from jax.experimental.pallas import tpu as pltpu
 from jax.sharding import PartitionSpec as P
 
 D = 8192
@@ -12,8 +15,289 @@
 epsilon = 1e-05
 grad_scale = 32.0
 
-
-def per_device(clip_feats, proj_weight):
+MESH = pl.DeviceIdType.MESH
+DMA = pltpu.SemaphoreType.DMA
+
+
+def remote(src, dst, send_sem, recv_sem, dp, feat):
+    return pltpu.make_async_remote_copy(
+        src_ref=src,
+        dst_ref=dst,
+        send_sem=send_sem,
+        recv_sem=recv_sem,
+        device_id=(dp, feat),
+        device_id_type=MESH,
+    )
+
+
+def rows_kernel(n, parts, x_ref, out_ref, send_a, recv_a, send_b, recv_b, send_c, recv_c):
+    z, f = lax.axis_index("dp"), lax.axis_index("feat")
+    q, c = lax.div(f, parts), lax.rem(f, parts)
+    for p in range(n):
+        own = jnp.logical_and(z == q, q == p)
+
+        @pl.when(own)
+        def _(p=p):
+            out_ref[c, p, z] = x_ref[p]
+
+        @pl.when(jnp.logical_not(own))
+        def _(p=p):
+            remote(x_ref.at[p], out_ref.at[c, p, z], send_a.at[p], recv_a.at[z], q, p * parts + c).start()
+
+    for s in range(n):
+
+        @pl.when(jnp.logical_not(jnp.logical_and(z == q, z == s)))
+        def _(s=s):
+            remote(x_ref.at[0], out_ref.at[c, q, s], send_a.at[0], recv_a.at[s], z, f).wait_recv()
+
+    def across(d, where):
+        block = out_ref.at[c, where]
+        return [
+            remote(block, block, send_c.at[e, d], recv_c.at[e, d], z, q * parts + lax.rem(c + e, parts))
+            for e in range(1, parts)
+        ]
+
+    mine = out_ref.at[c, q]
+    ring = [
+        remote(mine, mine, send_b.at[d], recv_b.at[d], z, lax.rem(q + d, n) * parts + c)
+        for d in range(1, n)
+    ]
+    for copy in ring:
+        copy.start()
+    pairs = across(0, q)
+    for copy in pairs:
+        copy.start()
+    for d in range(1, n):
+        ring[d - 1].wait_recv()
+        passed = across(d, lax.rem(q + n - d, n))
+        for copy in passed:
+            copy.start()
+        pairs += passed
+    for copy in pairs:
+        copy.wait()
+    for copy in ring:
+        copy.wait_send()
+    for p in range(n):
+
+        @pl.when(jnp.logical_not(jnp.logical_and(z == q, q == p)))
+        def _(p=p):
+            remote(x_ref.at[p], out_ref.at[c, p, z], send_a.at[p], recv_a.at[z], q, p * parts + c).wait_send()
+
+
+def gram_kernel(
+    n, m, g_ref, s_ref, out_ref, total_ref, plane, scalars, mid, scalar_mid, column, scalar_column,
+    send_a, recv_a, send_b, recv_b, send_c, recv_c, send_d, recv_d, send_e, recv_e,
+):
+    z, f = lax.axis_index("dp"), lax.axis_index("feat")
+    started = []
+    for d in range(1, m):
+        to = lax.rem(f + d, m)
+        started.append(remote(g_ref.at[to], plane.at[f], send_a.at[d], recv_a.at[d], z, to))
+        started.append(remote(s_ref, scalars.at[f], send_b.at[d], recv_b.at[d], z, to))
+    for copy in started:
+        copy.start()
+    plane[f] = g_ref[f]
+    scalars[f] = s_ref[...]
+    for copy in started:
+        copy.wait()
+    total = plane[0].astype(jnp.float32)
+    for i in range(1, m):
+        total += plane[i].astype(jnp.float32)
+    mid[...] = total.astype(mid.dtype)
+    small = scalars[0]
+    for i in range(1, m):
+        small += scalars[i]
+    scalar_mid[...] = small
+    started = []
+    for d in range(1, n):
+        to = lax.rem(z + d, n)
+        started.append(remote(mid, column.at[z], send_c.at[d], recv_c.at[d], to, f))
+        started.append(remote(scalar_mid, scalar_column.at[z], send_d.at[d], recv_d.at[d], to, f))
+    for copy in started:
+        copy.start()
+    column[z] = mid[...]
+    scalar_column[z] = scalar_mid[...]
+    for copy in started:
+        copy.wait()
+    total = column[0].astype(jnp.float32)
+    for i in range(1, n):
+        total += column[i].astype(jnp.float32)
+    out_ref[f] = total.astype(out_ref.dtype)
+    small = scalar_column[0]
+    for i in range(1, n):
+        small += scalar_column[i]
+    total_ref[...] = small
+    started = [
+        remote(out_ref.at[f], out_ref.at[f], send_e.at[d], recv_e.at[d], z, lax.rem(f + d, m))
+        for d in range(1, m)
+    ]
+    for copy in started:
+        copy.start()
+    for copy in started:
+        copy.wait()
+
+
+def column_kernel(n, x_ref, out_ref, send_up, recv_up, send_down, recv_down):
+    z, f = lax.axis_index("dp"), lax.axis_index("feat")
+
+    def up(d):
+        where = out_ref.at[z - d]
+        return remote(x_ref if d == 0 else where, where, send_up.at[d], recv_up.at[d], z + 1, f)
+
+    def down(d):
+        where = out_ref.at[z + d]
+        return remote(x_ref if d == 0 else where, where, send_down.at[d], recv_down.at[d], z - 1, f)
+
+    for d in range(n - 1):
+        if d > 0:
+
+            @pl.when(z >= d)
+            def _(d=d):
+                remote(x_ref, out_ref.at[z - d], send_up.at[0], recv_up.at[d - 1], z, f).wait_recv()
+
+        @pl.when(jnp.logical_and(z >= d, z < n - 1))
+        def _(d=d):
+            up(d).start()
+
+        if d > 0:
+
+            @pl.when(z + d < n)
+            def _(d=d):
+                remote(x_ref, out_ref.at[z + d], send_down.at[0], recv_down.at[d - 1], z, f).wait_recv()
+
+        @pl.when(jnp.logical_and(z + d < n, z > 0))
+        def _(d=d):
+            down(d).start()
+
+    out_ref[z] = x_ref[...]
+
+    @pl.when(z == n - 1)
+    def _():
+        remote(x_ref, out_ref.at[z - (n - 1)], send_up.at[0], recv_up.at[n - 2], z, f).wait_recv()
+
+    @pl.when(z == 0)
+    def _():
+        remote(x_ref, out_ref.at[z + (n - 1)], send_down.at[0], recv_down.at[n - 2], z, f).wait_recv()
+
+    for d in range(n - 1):
+
+        @pl.when(jnp.logical_and(z >= d, z < n - 1))
+        def _(d=d):
+            up(d).wait_send()
+
+        @pl.when(jnp.logical_and(z + d < n, z > 0))
+        def _(d=d):
+            down(d).wait_send()
+
+
+def call(kernel, outs, scratch, name, *args):
+    return pl.pallas_call(
+        kernel,
+        out_shape=outs,
+        in_specs=[pl.BlockSpec(memory_space=pltpu.VMEM)] * len(args),
+        out_specs=jax.tree.map(lambda _: pl.BlockSpec(memory_space=pltpu.VMEM), outs),
+        scratch_shapes=scratch,
+        compiler_params=pltpu.CompilerParams(has_side_effects=True, vmem_limit_bytes=32 * 2**20),
+        name=name,
+    )(*args)
+
+
+def by_kernels(clip_feats, proj_weight):
+    pairs = clip_feats.shape[1]
+    width = clip_feats.shape[2]
+    depth = proj_weight.shape[0]
+    n, m = lax.axis_size("dp"), lax.axis_size("feat")
+    parts = m // n
+    total = pairs * n
+    pair_count = float(total)
+    columns = width // n
+    piece = 2 * pairs // n
+    f32, bf16 = jnp.float32, jnp.bfloat16
+    rows = call(
+        functools.partial(rows_kernel, n, parts),
+        jax.ShapeDtypeStruct((parts, n, n, piece, width), bf16),
+        [DMA((n,))] * 4 + [DMA((parts, n))] * 2,
+        "rows",
+        clip_feats.reshape(n, piece, width),
+    ).reshape(parts, 2 * total, width)
+    partial = sum(
+        jnp.dot(rows[i], proj_weight[i * width : (i + 1) * width], preferred_element_type=f32)
+        for i in range(parts)
+    ).reshape(2, total, width)
+    partial = (partial - jnp.mean(partial, axis=1, keepdims=True)).astype(bf16)
+    pieces = jnp.stack([partial[:, :, i * columns : (i + 1) * columns] for i in range(n)])
+    pieces = lax.all_to_all(pieces, "dp", split_axis=0, concat_axis=0, tiled=True)
+    centered = jnp.sum(pieces.astype(f32), axis=0)
+    col_var = jnp.mean(centered * centered, axis=1, keepdims=True)
+    col_scale = lax.rsqrt(col_var + epsilon)
+    normed = centered * col_scale
+    quantized = normed.astype(bf16)
+    widened = quantized.astype(f32)
+    gram_part = jnp.einsum("vpc,vnc->vpn", quantized, quantized, preferred_element_type=f32)
+    diag_corr = jnp.sum(widened[0] * widened[1], axis=0) / pair_count
+    diag_part = jnp.sum((1.0 - diag_corr) ** 2 - off_weight * diag_corr * diag_corr)
+    square_part = jnp.sum(diag_corr * diag_corr)
+    lane = lax.broadcasted_iota(jnp.int32, (8, 128), 1)
+    small = jnp.where(lane == 0, diag_part, jnp.where(lane == 1, square_part, 0.0))
+    block = 2 * total // m
+    gram_q, small = call(
+        functools.partial(gram_kernel, n, m),
+        (jax.ShapeDtypeStruct((m, block, total), bf16), jax.ShapeDtypeStruct((8, 128), f32)),
+        [
+            pltpu.VMEM((m, block, total), bf16),
+            pltpu.VMEM((m, 8, 128), f32),
+            pltpu.VMEM((block, total), bf16),
+            pltpu.VMEM((8, 128), f32),
+            pltpu.VMEM((n, block, total), bf16),
+            pltpu.VMEM((n, 8, 128), f32),
+        ]
+        + [DMA((m,))] * 4
+        + [DMA((n,))] * 4
+        + [DMA((m,))] * 2,
+        "grams",
+        gram_part.astype(bf16).reshape(m, block, total),
+        small,
+    )
+    gram_q = gram_q.reshape(2, total, total)
+    slope = -2.0 * (1.0 - diag_corr) - 2.0 * off_weight * diag_corr
+    coefficient = 2.0 * off_weight / (pair_count * pair_count)
+    cross_first = jnp.dot(gram_q[1], quantized[0], preferred_element_type=f32)
+    cross_second = jnp.dot(gram_q[0], quantized[1], preferred_element_type=f32)
+    grad_norm = jnp.stack(
+        [
+            slope * widened[1] / pair_count + coefficient * cross_first,
+            slope * widened[0] / pair_count + coefficient * cross_second,
+        ]
+    )
+    mean_one = jnp.mean(grad_norm, axis=1, keepdims=True)
+    mean_two = jnp.mean(grad_norm * normed, axis=1, keepdims=True)
+    pre_q = (col_scale * (grad_norm - mean_one - normed * mean_two)).astype(bf16)
+    flat_grad = call(
+        functools.partial(column_kernel, n),
+        jax.ShapeDtypeStruct((n, 2 * total, columns), bf16),
+        [DMA((n,))] * 4,
+        "columns",
+        pre_q.reshape(2 * total, columns),
+    )
+    flat_grad = jnp.concatenate([flat_grad[i] for i in range(n)], axis=1)
+    summed = jnp.einsum("crk,rw->ckw", rows, flat_grad, preferred_element_type=f32)
+    weight_grad = grad_scale * summed.reshape(depth, width)
+    grams = gram_q.astype(f32)
+    frob_scaled = jnp.sum(grams[0] * grams[1]) / (pair_count * pair_count)
+    loss_value = 16.0 * (small[0, 0] + off_weight * frob_scaled) / float(D)
+    redundancy = 8.0 * pair_count * (frob_scaled - small[0, 1]) / (float(D) * float(D))
+    half = n // 2
+    z = lax.axis_index("dp")
+    own = grams.reshape(2, half, n, piece, total)
+    own = lax.dynamic_slice_in_dim(own, z, 1, axis=2)
+    own = (own[0] + own[1]).reshape(pairs, half, n, piece).transpose(0, 2, 1, 3).reshape(pairs, total)
+    row_ids = lax.broadcasted_iota(jnp.int32, (pairs, total), 0) + z * pairs
+    col_ids = lax.broadcasted_iota(jnp.int32, (pairs, total), 1)
+    pair_similarity = jnp.where(row_ids == col_ids, 0.0, own / (2.0 * math.sqrt(float(D))))
+    return (loss_value, weight_grad, redundancy, pair_similarity)
+
+
+def by_collectives(clip_feats, proj_weight):
     pairs = clip_feats.shape[1]
     width = clip_feats.shape[2]
     depth = proj_weight.shape[0]
@@ -78,6 +362,15 @@
     return (loss_value, grad_scale * summed, redundancy, pair_similarity)
 
 
+def per_device(clip_feats, proj_weight):
+    pairs, width = clip_feats.shape[1:]
+    n, m = lax.axis_size("dp"), lax.axis_size("feat")
+    aligned = n % 2 == 0 and m % n == 0 and m > n and proj_weight.shape[0] == width * (m // n)
+    aligned = aligned and width % (128 * n) == 0 and (2 * pairs) % (16 * n) == 0
+    aligned = aligned and (2 * pairs * n) % (16 * m) == 0
+    return (by_kernels if aligned else by_collectives)(clip_feats, proj_weight)
+
+
 def solution(mesh):
     placed = (P(None, "dp", "feat"), P("dp", "feat"))
     return jax.shard_map(

time: 369 us -> 206 us (0.56)
  blocking collectives: 158 us -> 0 us
  waiting for transfers between devices: 166 us -> 37.6 us
  Pallas kernels: 0 us -> 120 us
  between operations: 18.8 us -> 5.7 us
  other arithmetic: 10.2 us -> 15.6 us
  starting transfers between devices: 0.12 us -> 4.99 us
  local copies, waits for them, and re-layouts: 3.5 us -> 7.96 us
    psum x1 -> x0, waiting for transfers between devices: 129 us -> none  [per_device(): lax.psum((gram_part, diag_part, square_part), ('dp', 'feat'))]
    pallas_call x0 -> x3, Pallas kernels: none -> 120 us  [call(): pl.pallas_call(kernel, out_shape=outs, in_specs=[pl.BlockSpec(memory_spac...]
    all_to_all x2 -> x0, blocking collectives: 115 us -> none  [the longest x1 75.7 us: per_device(): lax.all_to_all(gathered, 'dp', split_axis=0, concat_axis=0, tiled=True)]
    psum x1 -> x0, blocking collectives: 43.1 us -> none  [per_device(): lax.psum((gram_part, diag_part, square_part), ('dp', 'feat'))]
    all_to_all x0 -> x1, waiting for transfers between devices: none -> 37.6 us  [by_kernels(): lax.all_to_all(pieces, 'dp', split_axis=0, concat_axis=0, tiled=True)]
    all_gather x2 -> x0, waiting for transfers between devices: 37 us -> none  [the longest x1 37 us: per_device(): gathered = lax.all_gather(clip_feats, 'feat', axis=0, tiled=False)]
    all_to_all x0 -> x1, starting transfers between devices: none -> 4.99 us  [by_kernels(): lax.all_to_all(pieces, 'dp', split_axis=0, concat_axis=0, tiled=True)]
    mul x1 -> x0, other arithmetic: 4.38 us -> none  [per_device(): return (loss_value, grad_scale * summed, redundancy, pair_similarity)]
  transfers between devices with their start and end apart: 3 -> 1, of which waited for: 2 -> 1; matrix products, arithmetic and copies ran while one was open for 1% -> 0% of each run, Pallas kernels for 0% -> 0%
where the time goes in v2:
time: 206 us; the launch traced here: 205 us
  Pallas kernels  120 us (58%)
  waiting for transfers between devices  37.6 us (18%)
  other arithmetic  15.6 us (8%)
  matrix products  13.2 us (6%)
  local copies, waits for them, and re-layouts  7.96 us (4%)
  between operations  5.7 us (3%)
  starting transfers between devices  4.99 us (2%)
    pallas_call x3, Pallas kernels, call(): pl.pallas_call(kernel, out_shape=outs, in_specs=[pl.BlockSpec(memory_spac...  120 us
    all_to_all x1, waiting for transfers between devices, by_kernels(): lax.all_to_all(pieces, 'dp', split_axis=0, concat_axis=0, tiled=True)  37.6 us
    dot_general x1, matrix products, by_kernels(): jnp.einsum('crk,rw->ckw', rows, flat_grad, preferred_element_type=f32)  7.02 us
    dot_general x2, matrix products, by_kernels(): jnp.dot(rows[i], proj_weight[i * width:(i + 1) * width], preferred_elemen...  5.29 us
    all_to_all x1, starting transfers between devices, by_kernels(): lax.all_to_all(pieces, 'dp', split_axis=0, concat_axis=0, tiled=True)  4.99 us
  transfers between devices with their start and end apart: 1, of which 1 were waited for; matrix products, arithmetic and copies ran while one was open for 0% of the time, Pallas kernels for 0%

profile of v2, /device:TPU:0, one launch (start us, length us, event | category | flops | bytes accessed | tf_op | source)
XLA Modules:
  0.0 205.3 jit_solution(14551226316917214972)
XLA Ops:
  0.6 1.0 copy-done
  1.6 54.2 %rows.1 = bf16[2,4,4,48,1024]{4,3,2,1,0:T(8,128)(2,1)S(1)} custom-call(bf16[4,48,1024]{2,1,0:T(8,128)(2,1)S(1)} %bitcast.99), custom_call_target="tpu_custom_call" | custom-call | tf_op jit(solution)/shard_map/rows/pallas_call | solution.py:194
  55.8 0.4 fusion.27
  56.2 1.8 copy-done.3
  58.0 1.8 fusion
  59.8 3.5 %fusion.4 = f32[768,1024]{1,0:T(8,128)} fusion(f32[768,1024]{1,0:T(8,128)S(1)} %fusion, bf16[768,1024]{1,0:T(8,128)(2,1)S(1)} %bitcast.104, bf16[2048,1024]{1,0:T(8,128)(2,1)S(1)} %copy-done.3), kind=kOutput, calls=%fused_computation.7 | convolution fusion | flops 1611399168 | bytes 9961472 | tf_op jit(solution)/shard_map/dot_general | solution.py:224
  63.3 2.1 %reduce_sum.83 = f32[2,1024]{1,0:T(2,128)S(1)} reduce(f32[2,384,1024]{2,1,0:T(8,128)} %bitcast.100, f32[]{:T(128)} %constant.19.clone.1), dimensions={1}, to_apply=%region_0.0 | reduce | flops 784384 | bytes 3153924 | tf_op jit(solution)/shard_map/reduce_sum | solution.py:227
  65.4 2.3 %subtract_convert_fusion = bf16[2,384,1024]{2,1,0:T(8,128)(2,1)S(1)} fusion(f32[2,384,1024]{2,1,0:T(8,128)} %bitcast.101, f32[2,1024]{1,0:T(2,128)S(1)} %broadcast_multiply_fusion.1), kind=kLoop, calls=%fused_computation.2 | loop fusion | flops 1572864 | bytes 4726784 | tf_op jit(solution)/shard_map/convert_element_type | solution.py:227
  67.8 1.3 pad_maximum_fusion
  69.2 5.0 %all-to-all-start = ((bf16[4,2,384,256]{3,2,1,0:T(8,128)(2,1)}), bf16[4,2,384,256]{3,2,1,0:T(8,128)(2,1)}, u32[]{:S(2)}, u32[]{:S(2)}) async-start(bf16[4,2,384,256]{3,2,1,0:T(8,128)(2,1)} %pad_maximum_fusion), calls=%async_computation | async-start | bytes 3145728 | tf_op jit(solution)/shard_map/all_to_all | solution.py:229
  74.2 37.6 %all-to-all-done = bf16[4,2,384,256]{3,2,1,0:T(8,128)(2,1)} async-done(((bf16[4,2,384,256]{3,2,1,0:T(8,128)(2,1)}), bf16[4,2,384,256]{3,2,1,0:T(8,128)(2,1)}, u32[]{:S(2)}, u32[]{:S(2)}) %all-to-all-start) | async-done | bytes 1572896 | tf_op jit(solution)/shard_map/all_to_all | solution.py:229
  111.7 1.7 convert_reduce_fusion
  113.8 0.6 subtract_reduce_fusion
  114.4 0.6 compare_select_fusion
  115.0 0.4 convolution_convert_fusion
  115.4 0.7 broadcast_select_fusion.s_ref
  116.0 29.8 %grams.1 = (bf16[8,96,384]{2,1,0:T(8,128)(2,1)S(1)}, f32[8,128]{1,0:T(8,128)S(1)}) custom-call(bf16[8,96,384]{2,1,0:T(8,128)(2,1)S(1)} %bitcast.98, f32[8,128]{1,0:T(8,128)S(1)} %broadcast_select_fusion.s_ref), custom_call_target="tpu_custom_call" | custom-call | tf_op jit(solution)/shard_map/grams/pallas_call | solution.py:194
  146.0 0.7 fusion.29
  146.7 0.3 fusion.16
  146.9 0.3 fusion.14
  147.2 0.1 multiply_reduce_fusion
  147.3 1.0 fusion.21
  148.3 0.8 fusion.20
  150.4 1.7 fusion.24
  152.0 1.3 div.62
  153.3 0.9 copy.10
  154.1 0.9 bitcast_select_fusion
  155.1 0.8 copy.11
  155.9 1.5 fusion.19.x_ref
  157.4 36.2 %columns.1 = bf16[4,768,256]{2,1,0:T(8,128)(2,1)S(1)} custom-call(bf16[768,256]{1,0:T(8,128)(2,1)S(1)} %fusion.19.x_ref), custom_call_target="tpu_custom_call" | custom-call | tf_op jit(solution)/shard_map/columns/pallas_call | solution.py:194
  193.6 1.0 slice_bitcast_fusion.9
  196.0 7.0 %broadcast_multiply_fusion = f32[1024,2,1024]{0,2,1:T(8,128)} fusion(bf16[2,768,1024]{2,1,0:T(8,128)(2,1)S(1)} %bitcast.97, bf16[768,256]{1,0:T(8,128)(2,1)} %get-tuple-element.21, bf16[768,256]{1,0:T(8,128)(2,1)} %get-tuple-element.22, bf16[768,256]{1,0:T(8,128)(2,1)} %get-tuple-element.23, bf16[768,256]{1,0:T(8,128)(2,1)S(1)} %get-tuple-element.20), kind=kOutput, calls=%fused_computation | convolution fusion | flops 3229614080 | bytes 13107200 | tf_op jit(solution)/shard_map/crk,rw->ckw/dot_general | solution.py:283
  (17 shorter events, 0.5 us)
Async XLA Ops:
  0.6 1.0 copy-start
  55.8 2.2 %copy-start.3 = (bf16[2048,1024]{1,0:T(8,128)(2,1)S(1)}, bf16[2048,1024]{1,0:T(8,128)(2,1)}, u32[]{:S(2)}) copy-start(bf16[2048,1024]{1,0:T(8,128)(2,1)} %param.3) | copy-start | bytes 12582916
  69.2 42.6 %all-to-all-start = ((bf16[4,2,384,256]{3,2,1,0:T(8,128)(2,1)}), bf16[4,2,384,256]{3,2,1,0:T(8,128)(2,1)}, u32[]{:S(2)}, u32[]{:S(2)}) async-start(bf16[4,2,384,256]{3,2,1,0:T(8,128)(2,1)} %pad_maximum_fusion), calls=%async_computation | async-start | bytes 3145728 | tf_op jit(solution)/shard_map/all_to_all | solution.py:229
  113.5 33.7 %copy-start.1 = (f32[2,384,256]{2,1,0:T(8,128)}, f32[2,384,256]{2,1,0:T(8,128)S(1)}, u32[]{:S(2)}) copy-start(f32[2,384,256]{2,1,0:T(8,128)S(1)} %convert_reduce_fusion) | copy-start | bytes 2359300
  146.0 2.3 %copy-start.2 = (f32[8,96,384]{2,1,0:T(8,128)}, f32[8,96,384]{2,1,0:T(8,128)S(1)}, u32[]{:S(2)}) copy-start(f32[8,96,384]{2,1,0:T(8,128)S(1)} %convert_element_type.34) | copy-start | bytes 3538948

commit v3 on v2

--- a/solution.py
+++ b/solution.py
@@ -14,6 +14,7 @@
 off_weight = 0.0051
 epsilon = 1e-05
 grad_scale = 32.0
+cuts = 4
 
 MESH = pl.DeviceIdType.MESH
 DMA = pltpu.SemaphoreType.DMA
@@ -30,58 +31,122 @@
     )
 
 
-def rows_kernel(n, parts, x_ref, out_ref, send_a, recv_a, send_b, recv_b, send_c, recv_c):
+def rows_kernel(
+    n, parts, x_ref, out_ref, mid, local, send_a, recv_a, send_b, recv_b, send_c, recv_c, send_d, recv_d
+):
     z, f = lax.axis_index("dp"), lax.axis_index("feat")
     q, c = lax.div(f, parts), lax.rem(f, parts)
-    for p in range(n):
-        own = jnp.logical_and(z == q, q == p)
-
-        @pl.when(own)
-        def _(p=p):
-            out_ref[c, p, z] = x_ref[p]
-
-        @pl.when(jnp.logical_not(own))
-        def _(p=p):
-            remote(x_ref.at[p], out_ref.at[c, p, z], send_a.at[p], recv_a.at[z], q, p * parts + c).start()
-
-    for s in range(n):
-
-        @pl.when(jnp.logical_not(jnp.logical_and(z == q, z == s)))
+    spread = []
+    for d in range(1, n):
+        to = lax.rem(q + d, n)
+        spread.append(remote(x_ref.at[to], mid.at[q], send_a.at[d], recv_a.at[d], z, to * parts + c))
+    for copy in spread:
+        copy.start()
+    kept = pltpu.make_async_copy(x_ref.at[q], mid.at[q], local.at[0])
+    kept.start()
+    kept.wait()
+    for d in range(n):
+        s = lax.rem(q + n - d, n)
+        if d > 0:
+            spread[d - 1].wait_recv()
+
+        @pl.when(z != s)
+        def _(d=d, s=s):
+            remote(mid.at[s], out_ref.at[c, q, z], send_b.at[d], recv_b.at[z], s, f).start()
+
+        @pl.when(z == s)
         def _(s=s):
-            remote(x_ref.at[0], out_ref.at[c, q, s], send_a.at[0], recv_a.at[s], z, f).wait_recv()
-
-    def across(d, where):
-        block = out_ref.at[c, where]
+            own = pltpu.make_async_copy(mid.at[s], out_ref.at[c, q, z], local.at[1])
+            own.start()
+            own.wait()
+
+    def across(d, e):
+        block = out_ref.at[c, lax.rem(q + n - d, n), lax.rem(z + e, n)]
         return [
-            remote(block, block, send_c.at[e, d], recv_c.at[e, d], z, q * parts + lax.rem(c + e, parts))
-            for e in range(1, parts)
+            remote(block, block, send_d.at[i, d, e], recv_d.at[i, d, e], z, q * parts + lax.rem(c + i, parts))
+            for i in range(1, parts)
         ]
 
-    mine = out_ref.at[c, q]
-    ring = [
-        remote(mine, mine, send_b.at[d], recv_b.at[d], z, lax.rem(q + d, n) * parts + c)
-        for d in range(1, n)
-    ]
-    for copy in ring:
-        copy.start()
-    pairs = across(0, q)
-    for copy in pairs:
-        copy.start()
-    for d in range(1, n):
-        ring[d - 1].wait_recv()
-        passed = across(d, lax.rem(q + n - d, n))
+    ring, pairs = {}, []
+    for e in range(n):
+        s = lax.rem(z + e, n)
+        mine = out_ref.at[c, q, s]
+        if e > 0:
+            remote(x_ref.at[0], mine, send_b.at[0], recv_b.at[s], z, f).wait_recv()
+        for d in range(1, n):
+            to = lax.rem(q + d, n) * parts + c
+            ring[d, e] = remote(mine, mine, send_c.at[d, e], recv_c.at[d, e], z, to)
+            ring[d, e].start()
+        passed = across(0, e)
         for copy in passed:
             copy.start()
         pairs += passed
+    for e in range(n):
+        for d in range(1, n):
+            ring[d, e].wait_recv()
+            passed = across(d, e)
+            for copy in passed:
+                copy.start()
+            pairs += passed
     for copy in pairs:
         copy.wait()
-    for copy in ring:
+    for copy in list(ring.values()) + spread:
         copy.wait_send()
-    for p in range(n):
-
-        @pl.when(jnp.logical_not(jnp.logical_and(z == q, q == p)))
-        def _(p=p):
-            remote(x_ref.at[p], out_ref.at[c, p, z], send_a.at[p], recv_a.at[z], q, p * parts + c).wait_send()
+    for d in range(n):
+        s = lax.rem(q + n - d, n)
+
+        @pl.when(z != s)
+        def _(d=d, s=s):
+            remote(mid.at[s], out_ref.at[c, q, z], send_b.at[d], recv_b.at[z], s, f).wait_send()
+
+
+def sums_kernel(n, k, x_ref, out_ref, sums, above, below, send_up, recv_up, send_down, recv_down):
+    z, f = lax.axis_index("dp"), lax.axis_index("feat")
+
+    def step(t, i, start, rising):
+        first = z == (0 if rising else n - 1)
+        active = z < t if rising else z > t
+        got = below if rising else above
+        send, recv = (send_up, recv_up) if rising else (send_down, recv_down)
+        to = z + 1 if rising else z - 1
+
+        @pl.when(jnp.logical_and(active, first))
+        def _():
+            copy = remote(x_ref.at[t, i], got.at[t, i], send.at[t, i], recv.at[t, i], to, f)
+            copy.start() if start else copy.wait_send()
+
+        @pl.when(jnp.logical_and(active, jnp.logical_not(first)))
+        def _():
+            copy = remote(sums.at[t, i], got.at[t, i], send.at[t, i], recv.at[t, i], to, f)
+            if start:
+                copy.wait_recv()
+                total = x_ref[t, i].astype(jnp.float32) + got[t, i].astype(jnp.float32)
+                sums[t, i] = total.astype(sums.dtype)
+                copy.start()
+            else:
+                copy.wait_send()
+
+    for j in range(n - 1):
+        for i in range(k):
+            step(n - 1 - j, i, True, True)
+            step(j, i, True, False)
+    out_ref[...] = x_ref[z].astype(jnp.float32)
+    for i in range(k):
+
+        @pl.when(z > 0)
+        def _(i=i):
+            remote(x_ref.at[0, i], below.at[z, i], send_up.at[0, i], recv_up.at[z, i], z, f).wait_recv()
+            out_ref[i] += below[z, i].astype(jnp.float32)
+
+        @pl.when(z < n - 1)
+        def _(i=i):
+            remote(x_ref.at[0, i], above.at[z, i], send_down.at[0, i], recv_down.at[z, i], z, f).wait_recv()
+            out_ref[i] += above[z, i].astype(jnp.float32)
+
+    for j in range(n - 1):
+        for i in range(k):
+            step(n - 1 - j, i, False, True)
+            step(j, i, False, False)
 
 
 def gram_kernel(
@@ -137,57 +202,54 @@
         copy.wait()
 
 
-def column_kernel(n, x_ref, out_ref, send_up, recv_up, send_down, recv_down):
+def column_kernel(n, k, x_ref, out_ref, send_up, recv_up, send_down, recv_down):
     z, f = lax.axis_index("dp"), lax.axis_index("feat")
 
-    def up(d):
-        where = out_ref.at[z - d]
-        return remote(x_ref if d == 0 else where, where, send_up.at[d], recv_up.at[d], z + 1, f)
-
-    def down(d):
-        where = out_ref.at[z + d]
-        return remote(x_ref if d == 0 else where, where, send_down.at[d], recv_down.at[d], z - 1, f)
+    def up(d, i):
+        where = out_ref.at[z - d, i]
+        src = x_ref.at[i] if d == 0 else where
+        return remote(src, where, send_up.at[d, i], recv_up.at[d, i], z + 1, f)
+
+    def down(d, i):
+        where = out_ref.at[z + d, i]
+        src = x_ref.at[i] if d == 0 else where
+        return remote(src, where, send_down.at[d, i], recv_down.at[d, i], z - 1, f)
+
+    def arrived(d, i):
+        @pl.when(z >= d)
+        def _():
+            remote(x_ref.at[i], out_ref.at[z - d, i], send_up.at[0, i], recv_up.at[d - 1, i], z, f).wait_recv()
+
+        @pl.when(z + d < n)
+        def _():
+            remote(x_ref.at[i], out_ref.at[z + d, i], send_down.at[0, i], recv_down.at[d - 1, i], z, f).wait_recv()
 
     for d in range(n - 1):
-        if d > 0:
-
-            @pl.when(z >= d)
-            def _(d=d):
-                remote(x_ref, out_ref.at[z - d], send_up.at[0], recv_up.at[d - 1], z, f).wait_recv()
-
-        @pl.when(jnp.logical_and(z >= d, z < n - 1))
-        def _(d=d):
-            up(d).start()
-
-        if d > 0:
-
-            @pl.when(z + d < n)
-            def _(d=d):
-                remote(x_ref, out_ref.at[z + d], send_down.at[0], recv_down.at[d - 1], z, f).wait_recv()
-
-        @pl.when(jnp.logical_and(z + d < n, z > 0))
-        def _(d=d):
-            down(d).start()
+        for i in range(k):
+            if d > 0:
+                arrived(d, i)
+
+            @pl.when(jnp.logical_and(z >= d, z < n - 1))
+            def _(d=d, i=i):
+                up(d, i).start()
+
+            @pl.when(jnp.logical_and(z + d < n, z > 0))
+            def _(d=d, i=i):
+                down(d, i).start()
 
     out_ref[z] = x_ref[...]
-
-    @pl.when(z == n - 1)
-    def _():
-        remote(x_ref, out_ref.at[z - (n - 1)], send_up.at[0], recv_up.at[n - 2], z, f).wait_recv()
-
-    @pl.when(z == 0)
-    def _():
-        remote(x_ref, out_ref.at[z + (n - 1)], send_down.at[0], recv_down.at[n - 2], z, f).wait_recv()
-
+    for i in range(k):
+        arrived(n - 1, i)
     for d in range(n - 1):
-
-        @pl.when(jnp.logical_and(z >= d, z < n - 1))
-        def _(d=d):
-            up(d).wait_send()
-
-        @pl.when(jnp.logical_and(z + d < n, z > 0))
-        def _(d=d):
-            down(d).wait_send()
+        for i in range(k):
+
+            @pl.when(jnp.logical_and(z >= d, z < n - 1))
+            def _(d=d, i=i):
+                up(d, i).wait_send()
+
+            @pl.when(jnp.logical_and(z + d < n, z > 0))
+            def _(d=d, i=i):
+                down(d, i).wait_send()
 
 
 def call(kernel, outs, scratch, name, *args):
@@ -216,7 +278,10 @@
     rows = call(
         functools.partial(rows_kernel, n, parts),
         jax.ShapeDtypeStruct((parts, n, n, piece, width), bf16),
-        [DMA((n,))] * 4 + [DMA((parts, n))] * 2,
+        [pltpu.VMEM((n, piece, width), bf16), DMA((2,))]
+        + [DMA((n,))] * 4
+        + [DMA((n, n))] * 2
+        + [DMA((parts, n, n))] * 2,
         "rows",
         clip_feats.reshape(n, piece, width),
     ).reshape(parts, 2 * total, width)
@@ -226,8 +291,14 @@
     ).reshape(2, total, width)
     partial = (partial - jnp.mean(partial, axis=1, keepdims=True)).astype(bf16)
     pieces = jnp.stack([partial[:, :, i * columns : (i + 1) * columns] for i in range(n)])
-    pieces = lax.all_to_all(pieces, "dp", split_axis=0, concat_axis=0, tiled=True)
-    centered = jnp.sum(pieces.astype(f32), axis=0)
+    k = cuts
+    centered = call(
+        functools.partial(sums_kernel, n, k),
+        jax.ShapeDtypeStruct((k, 2 * total // k, columns), f32),
+        [pltpu.VMEM((n, k, 2 * total // k, columns), bf16)] * 3 + [DMA((n, k))] * 4,
+        "sums",
+        pieces.reshape(n, k, 2 * total // k, columns),
+    ).reshape(2, total, columns)
     col_var = jnp.mean(centered * centered, axis=1, keepdims=True)
     col_scale = lax.rsqrt(col_var + epsilon)
     normed = centered * col_scale
@@ -273,12 +344,12 @@
     mean_two = jnp.mean(grad_norm * normed, axis=1, keepdims=True)
     pre_q = (col_scale * (grad_norm - mean_one - normed * mean_two)).astype(bf16)
     flat_grad = call(
-        functools.partial(column_kernel, n),
-        jax.ShapeDtypeStruct((n, 2 * total, columns), bf16),
-        [DMA((n,))] * 4,
+        functools.partial(column_kernel, n, k),
+        jax.ShapeDtypeStruct((n, k, 2 * total // k, columns), bf16),
+        [DMA((n, k))] * 4,
         "columns",
-        pre_q.reshape(2 * total, columns),
-    )
+        pre_q.reshape(k, 2 * total // k, columns),
+    ).reshape(n, 2 * total, columns)
     flat_grad = jnp.concatenate([flat_grad[i] for i in range(n)], axis=1)
     summed = jnp.einsum("crk,rw->ckw", rows, flat_grad, preferred_element_type=f32)
     weight_grad = grad_scale * summed.reshape(depth, width)
@@ -368,6 +439,7 @@
     aligned = n % 2 == 0 and m % n == 0 and m > n and proj_weight.shape[0] == width * (m // n)
     aligned = aligned and width % (128 * n) == 0 and (2 * pairs) % (16 * n) == 0
     aligned = aligned and (2 * pairs * n) % (16 * m) == 0
+    aligned = aligned and (2 * pairs * n) % (16 * cuts) == 0
     return (by_kernels if aligned else by_collectives)(clip_feats, proj_weight)
 
 

time: 206 us -> 171 us (0.83)
  waiting for transfers between devices: 37.6 us -> 0 us
  Pallas kernels: 120 us -> 144 us
  other arithmetic: 15.6 us -> 4.3 us
  starting transfers between devices: 4.99 us -> 0 us
  matrix products: 13.2 us -> 10.3 us
    all_to_all x1 -> x0, waiting for transfers between devices: 37.6 us -> none  [by_kernels(): lax.all_to_all(pieces, 'dp', split_axis=0, concat_axis=0, tiled=True)]
    pallas_call x3 -> x4, Pallas kernels: 120 us -> 144 us  [call(): pl.pallas_call(kernel, out_shape=outs, in_specs=[pl.BlockSpec(memory_spac...]
    all_to_all x1 -> x0, starting transfers between devices: 4.99 us -> none  [by_kernels(): lax.all_to_all(pieces, 'dp', split_axis=0, concat_axis=0, tiled=True)]
  transfers between devices with their start and end apart: 1 -> 0, of which waited for: 1 -> 0; matrix products, arithmetic and copies ran while one was open for 0% -> 0% of each run, Pallas kernels for 0% -> 0%
where the time goes in v3:
time: 171 us
  Pallas kernels  144 us (84%)
  matrix products  10.3 us (6%)
  local copies, waits for them, and re-layouts  6.56 us (4%)
  between operations  5.75 us (3%)
  other arithmetic  4.3 us (3%)
    pallas_call x4, Pallas kernels, call(): pl.pallas_call(kernel, out_shape=outs, in_specs=[pl.BlockSpec(memory_spac...  144 us
    dot_general x1, matrix products, by_kernels(): jnp.einsum('crk,rw->ckw', rows, flat_grad, preferred_element_type=f32)  5.79 us
    unnamed x9, local copies, waits for them, and re-layouts  4.71 us
    dot_general x2, matrix products, by_kernels(): jnp.dot(rows[i], proj_weight[i * width:(i + 1) * width], preferred_elemen...  3.63 us

profile of v3, /device:TPU:0, one launch (start us, length us, event | category | flops | bytes accessed | tf_op | source)
XLA Modules:
  0.0 170.5 jit_solution(6255420142407190432)
XLA Ops:
  0.7 1.0 copy-done.2
  1.7 35.3 %rows.1 = bf16[2,4,4,48,1024]{4,3,2,1,0:T(8,128)(2,1)S(1)} custom-call(bf16[4,48,1024]{2,1,0:T(8,128)(2,1)S(1)} %bitcast.81), custom_call_target="tpu_custom_call" | custom-call | tf_op jit(solution)/shard_map/rows/pallas_call | solution.py:256
  37.0 0.4 fusion.25
  37.4 1.3 copy-done
  38.7 1.7 copy-done.3
  40.4 1.8 %fusion = f32[768,1024]{1,0:T(8,128)S(1)} fusion(bf16[768,1024]{1,0:T(8,128)(2,1)S(1)} %bitcast.93, bf16[2048,1024]{1,0:T(8,128)(2,1)S(1)} %copy-done.3), kind=kOutput, calls=%fused_computation.2 | convolution fusion | flops 1610612736 | bytes 6815744 | tf_op jit(solution)/shard_map/dot_general | solution.py:289
  42.2 1.8 %fusion.4 = f32[768,1024]{1,0:T(8,128)S(1)} fusion(f32[768,1024]{1,0:T(8,128)S(1)} %fusion, bf16[768,1024]{1,0:T(8,128)(2,1)S(1)} %bitcast.92, bf16[2048,1024]{1,0:T(8,128)(2,1)S(1)} %copy-done.3), kind=kOutput, calls=%fused_computation.6 | convolution fusion | flops 1611399168 | bytes 9961472 | tf_op jit(solution)/shard_map/dot_general | solution.py:289
  44.0 0.2 reduce_sum.86
  44.2 0.4 subtract_convert_fusion
  44.6 0.1 fusion.27
  44.7 0.2 pad_maximum_fusion.x_ref
  44.9 42.3 %sums.1 = f32[4,192,256]{2,1,0:T(8,128)S(1)} custom-call(bf16[4,4,192,256]{3,2,1,0:T(8,128)(2,1)S(1)} %pad_maximum_fusion.x_ref), custom_call_target="tpu_custom_call" | custom-call | tf_op jit(solution)/shard_map/sums/pallas_call | solution.py:256
  87.4 0.1 fusion.23
  87.6 0.6 subtract_reduce_fusion
  88.2 0.6 compare_select_fusion
  88.9 0.7 broadcast_select_fusion.s_ref
  89.5 0.4 convolution_convert_fusion
  89.9 32.6 %grams.1 = (bf16[8,96,384]{2,1,0:T(8,128)(2,1)S(1)}, f32[8,128]{1,0:T(8,128)S(1)}) custom-call(bf16[8,96,384]{2,1,0:T(8,128)(2,1)S(1)} %bitcast.80, f32[8,128]{1,0:T(8,128)S(1)} %broadcast_select_fusion.s_ref), custom_call_target="tpu_custom_call" | custom-call | tf_op jit(solution)/shard_map/grams/pallas_call | solution.py:256
  122.5 0.6 fusion.29
  123.2 0.3 fusion.16
  123.4 0.3 fusion.14
  123.7 0.1 fusion.22
  123.9 0.1 multiply_reduce_fusion
  124.0 0.2 multiply_convert_fusion.x_ref
  124.2 0.1 convert_element_type.30
  124.3 0.8 fusion.18
  127.7 0.3 div.62
  128.0 0.2 copy.14
  128.2 0.8 copy.15
  129.0 33.3 %columns.1 = bf16[4,4,192,256]{3,2,1,0:T(8,128)(2,1)S(1)} custom-call(bf16[4,192,256]{2,1,0:T(8,128)(2,1)S(1)} %multiply_convert_fusion.x_ref), custom_call_target="tpu_custom_call" | custom-call | tf_op jit(solution)/shard_map/columns/pallas_call | solution.py:256
  162.3 0.1 fusion.26
  162.5 5.8 %broadcast_multiply_fusion = f32[1024,2,1024]{0,2,1:T(8,128)} fusion(bf16[2,768,1024]{2,1,0:T(8,128)(2,1)S(1)} %bitcast.79, bf16[768,256]{1,0:T(8,128)(2,1)S(1)} %bitcast.97, bf16[768,256]{1,0:T(8,128)(2,1)S(1)} %bitcast.98, bf16[768,256]{1,0:T(8,128)(2,1)S(1)} %bitcast.99, bf16[768,256]{1,0:T(8,128)(2,1)S(1)} %bitcast.96), kind=kOutput, calls=%fused_computation | convolution fusion | flops 3229614080 | bytes 13107200 | tf_op jit(solution)/shard_map/crk,rw->ckw/dot_general | solution.py:354
  (26 shorter events, 0.5 us)
Async XLA Ops:
  0.7 1.0 copy-start.2
  37.0 1.7 copy-start
  37.0 3.3 %copy-start.3 = (bf16[2048,1024]{1,0:T(8,128)(2,1)S(1)}, bf16[2048,1024]{1,0:T(8,128)(2,1)}, u32[]{:S(2)}) copy-start(bf16[2048,1024]{1,0:T(8,128)(2,1)} %param.3) | copy-start | bytes 12582916
  129.0 33.4 %copy-start.1 = (bf16[2,4,4,48,1024]{4,3,2,1,0:T(8,128)(2,1)S(1)}, bf16[2,4,4,48,1024]{4,3,2,1,0:T(8,128)(2,1)}, u32[]{:S(2)}) copy-start(bf16[2,4,4,48,1024]{4,3,2,1,0:T(8,128)(2,1)} %copy-done) | copy-start | bytes 9437188

commit v4 on v3

--- a/solution.py
+++ b/solution.py
@@ -113,7 +113,15 @@
         @pl.when(jnp.logical_and(active, first))
         def _():
             copy = remote(x_ref.at[t, i], got.at[t, i], send.at[t, i], recv.at[t, i], to, f)
-            copy.start() if start else copy.wait_send()
+            order = (n - 1 - t if rising else t) * k + i
+            if start:
+                copy.start()
+                if order >= 2:
+                    j, b = divmod(order - 2, k)
+                    a = n - 1 - j if rising else j
+                    remote(x_ref.at[a, b], got.at[a, b], send.at[a, b], recv.at[a, b], to, f).wait_send()
+            elif order >= (n - 1) * k - 2:
+                copy.wait_send()
 
         @pl.when(jnp.logical_and(active, jnp.logical_not(first)))
         def _():

time: 171 us -> 171 us (level)
  no operation moved by 1% of the time
where the time goes in v4:
time: 171 us; the launch traced here: 170 us
  Pallas kernels  144 us (84%)
  matrix products  10.3 us (6%)
  local copies, waits for them, and re-layouts  6.56 us (4%)
  between operations  5.75 us (3%)
  other arithmetic  4.3 us (3%)
    pallas_call x4, Pallas kernels, call(): pl.pallas_call(kernel, out_shape=outs, in_specs=[pl.BlockSpec(memory_spac...  144 us
    dot_general x1, matrix products, by_kernels(): jnp.einsum('crk,rw->ckw', rows, flat_grad, preferred_element_type=f32)  5.79 us
    unnamed x9, local copies, waits for them, and re-layouts  4.71 us
    dot_general x2, matrix products, by_kernels(): jnp.dot(rows[i], proj_weight[i * width:(i + 1) * width], preferred_elemen...  3.63 us

profile of v4, /device:TPU:0, one launch (start us, length us, event | category | flops | bytes accessed | tf_op | source)
XLA Modules:
  0.0 170.5 jit_solution(18275196275541646886)
XLA Ops:
  0.7 1.0 copy-done.2
  1.7 35.3 %rows.1 = bf16[2,4,4,48,1024]{4,3,2,1,0:T(8,128)(2,1)S(1)} custom-call(bf16[4,48,1024]{2,1,0:T(8,128)(2,1)S(1)} %bitcast.81), custom_call_target="tpu_custom_call" | custom-call | tf_op jit(solution)/shard_map/rows/pallas_call | solution.py:264
  37.0 0.4 fusion.25
  37.4 1.3 copy-done
  38.7 1.7 copy-done.3
  40.4 1.8 %fusion = f32[768,1024]{1,0:T(8,128)S(1)} fusion(bf16[768,1024]{1,0:T(8,128)(2,1)S(1)} %bitcast.93, bf16[2048,1024]{1,0:T(8,128)(2,1)S(1)} %copy-done.3), kind=kOutput, calls=%fused_computation.2 | convolution fusion | flops 1610612736 | bytes 6815744 | tf_op jit(solution)/shard_map/dot_general | solution.py:297
  42.2 1.8 %fusion.4 = f32[768,1024]{1,0:T(8,128)S(1)} fusion(f32[768,1024]{1,0:T(8,128)S(1)} %fusion, bf16[768,1024]{1,0:T(8,128)(2,1)S(1)} %bitcast.92, bf16[2048,1024]{1,0:T(8,128)(2,1)S(1)} %copy-done.3), kind=kOutput, calls=%fused_computation.6 | convolution fusion | flops 1611399168 | bytes 9961472 | tf_op jit(solution)/shard_map/dot_general | solution.py:297
  44.0 0.2 reduce_sum.86
  44.2 0.4 subtract_convert_fusion
  44.6 0.1 fusion.27
  44.7 0.2 pad_maximum_fusion.x_ref
  44.9 42.3 %sums.1 = f32[4,192,256]{2,1,0:T(8,128)S(1)} custom-call(bf16[4,4,192,256]{3,2,1,0:T(8,128)(2,1)S(1)} %pad_maximum_fusion.x_ref), custom_call_target="tpu_custom_call" | custom-call | tf_op jit(solution)/shard_map/sums/pallas_call | solution.py:264
  87.4 0.1 fusion.23
  87.6 0.6 subtract_reduce_fusion
  88.2 0.6 compare_select_fusion
  88.8 0.7 broadcast_select_fusion.s_ref
  89.5 0.4 convolution_convert_fusion
  89.9 32.6 %grams.1 = (bf16[8,96,384]{2,1,0:T(8,128)(2,1)S(1)}, f32[8,128]{1,0:T(8,128)S(1)}) custom-call(bf16[8,96,384]{2,1,0:T(8,128)(2,1)S(1)} %bitcast.80, f32[8,128]{1,0:T(8,128)S(1)} %broadcast_select_fusion.s_ref), custom_call_target="tpu_custom_call" | custom-call | tf_op jit(solution)/shard_map/grams/pallas_call | solution.py:264
  122.5 0.6 fusion.29
  123.2 0.3 fusion.16
  123.4 0.3 fusion.14
  123.7 0.1 fusion.22
  123.8 0.1 multiply_reduce_fusion
  124.0 0.2 multiply_convert_fusion.x_ref
  124.2 0.1 convert_element_type.30
  124.3 0.8 fusion.18
  127.7 0.3 div.62
  128.0 0.2 copy.14
  128.2 0.8 copy.15
  129.0 33.3 %columns.1 = bf16[4,4,192,256]{3,2,1,0:T(8,128)(2,1)S(1)} custom-call(bf16[4,192,256]{2,1,0:T(8,128)(2,1)S(1)} %multiply_convert_fusion.x_ref), custom_call_target="tpu_custom_call" | custom-call | tf_op jit(solution)/shard_map/columns/pallas_call | solution.py:264
  162.3 0.1 fusion.26
  162.4 5.8 %broadcast_multiply_fusion = f32[1024,2,1024]{0,2,1:T(8,128)} fusion(bf16[2,768,1024]{2,1,0:T(8,128)(2,1)S(1)} %bitcast.79, bf16[768,256]{1,0:T(8,128)(2,1)S(1)} %bitcast.97, bf16[768,256]{1,0:T(8,128)(2,1)S(1)} %bitcast.98, bf16[768,256]{1,0:T(8,128)(2,1)S(1)} %bitcast.99, bf16[768,256]{1,0:T(8,128)(2,1)S(1)} %bitcast.96), kind=kOutput, calls=%fused_computation | convolution fusion | flops 3229614080 | bytes 13107200 | tf_op jit(solution)/shard_map/crk,rw->ckw/dot_general | solution.py:362
  (26 shorter events, 0.5 us)
Async XLA Ops:
  0.7 1.0 copy-start.2
  37.0 1.7 copy-start
  37.0 3.3 %copy-start.3 = (bf16[2048,1024]{1,0:T(8,128)(2,1)S(1)}, bf16[2048,1024]{1,0:T(8,128)(2,1)}, u32[]{:S(2)}) copy-start(bf16[2048,1024]{1,0:T(8,128)(2,1)} %param.3) | copy-start | bytes 12582916
  129.0 33.4 %copy-start.1 = (bf16[2,4,4,48,1024]{4,3,2,1,0:T(8,128)(2,1)S(1)}, bf16[2,4,4,48,1024]{4,3,2,1,0:T(8,128)(2,1)}, u32[]{:S(2)}) copy-start(bf16[2,4,4,48,1024]{4,3,2,1,0:T(8,128)(2,1)} %copy-done) | copy-start | bytes 9437188

commit v5 on v4

--- a/solution.py
+++ b/solution.py
@@ -14,7 +14,7 @@
 off_weight = 0.0051
 epsilon = 1e-05
 grad_scale = 32.0
-cuts = 4
+cuts = 8
 
 MESH = pl.DeviceIdType.MESH
 DMA = pltpu.SemaphoreType.DMA

time: 171 us -> 192 us (1.12)
  Pallas kernels: 144 us -> 165 us
    pallas_call x4, Pallas kernels: 144 us -> 165 us  [call(): pl.pallas_call(kernel, out_shape=outs, in_specs=[pl.BlockSpec(memory_spac...]
where the time goes in v5:
time: 192 us
  Pallas kernels  165 us (86%)
  matrix products  10.3 us (5%)
  local copies, waits for them, and re-layouts  6.52 us (3%)
  between operations  5.78 us (3%)
  other arithmetic  4.32 us (2%)
    pallas_call x4, Pallas kernels, call(): pl.pallas_call(kernel, out_shape=outs, in_specs=[pl.BlockSpec(memory_spac...  165 us
    dot_general x1, matrix products, by_kernels(): jnp.einsum('crk,rw->ckw', rows, flat_grad, preferred_element_type=f32)  5.79 us
    unnamed x9, local copies, waits for them, and re-layouts  4.71 us

profile of v5, /device:TPU:0, one launch (start us, length us, event | category | flops | bytes accessed | tf_op | source)
XLA Modules:
  0.0 192.2 jit_solution(14432693479626867693)
XLA Ops:
  0.7 1.0 copy-done.2
  1.7 35.3 %rows.1 = bf16[2,4,4,48,1024]{4,3,2,1,0:T(8,128)(2,1)S(1)} custom-call(bf16[4,48,1024]{2,1,0:T(8,128)(2,1)S(1)} %bitcast.81), custom_call_target="tpu_custom_call" | custom-call | tf_op jit(solution)/shard_map/rows/pallas_call | solution.py:264
  37.0 0.4 fusion.25
  37.4 1.3 copy-done
  38.7 1.7 copy-done.3
  40.4 1.8 fusion
  42.2 1.8 fusion.4
  44.0 0.2 reduce_sum.86
  44.2 0.4 subtract_convert_fusion
  44.6 0.1 fusion.27
  44.7 0.2 pad_maximum_fusion.x_ref
  44.9 62.6 %sums.1 = f32[8,96,256]{2,1,0:T(8,128)S(1)} custom-call(bf16[4,8,96,256]{3,2,1,0:T(8,128)(2,1)S(1)} %pad_maximum_fusion.x_ref), custom_call_target="tpu_custom_call" | custom-call | tf_op jit(solution)/shard_map/sums/pallas_call | solution.py:264
  107.7 0.1 fusion.23
  107.8 0.6 subtract_reduce_fusion
  108.5 0.6 compare_select_fusion
  109.1 0.7 broadcast_select_fusion.s_ref
  109.8 0.4 convolution_convert_fusion
  110.1 33.5 %grams.1 = (bf16[8,96,384]{2,1,0:T(8,128)(2,1)S(1)}, f32[8,128]{1,0:T(8,128)S(1)}) custom-call(bf16[8,96,384]{2,1,0:T(8,128)(2,1)S(1)} %bitcast.80, f32[8,128]{1,0:T(8,128)S(1)} %broadcast_select_fusion.s_ref), custom_call_target="tpu_custom_call" | custom-call | tf_op jit(solution)/shard_map/grams/pallas_call | solution.py:264
  143.6 0.6 fusion.29
  144.3 0.3 fusion.16
  144.5 0.3 fusion.14
  144.8 0.1 fusion.22
  144.9 0.1 multiply_reduce_fusion
  145.1 0.2 multiply_convert_fusion.x_ref
  145.3 0.1 convert_element_type.30
  145.4 0.8 fusion.18
  148.8 0.3 div.62
  149.1 0.2 copy.14
  149.3 0.8 copy.15
  150.1 33.9 %columns.1 = bf16[4,8,96,256]{3,2,1,0:T(8,128)(2,1)S(1)} custom-call(bf16[8,96,256]{2,1,0:T(8,128)(2,1)S(1)} %multiply_convert_fusion.x_ref), custom_call_target="tpu_custom_call" | custom-call | tf_op jit(solution)/shard_map/columns/pallas_call | solution.py:264
  184.0 0.1 fusion.26
  184.1 5.8 %broadcast_multiply_fusion = f32[1024,2,1024]{0,2,1:T(8,128)} fusion(bf16[2,768,1024]{2,1,0:T(8,128)(2,1)S(1)} %bitcast.79, bf16[768,256]{1,0:T(8,128)(2,1)S(1)} %bitcast.97, bf16[768,256]{1,0:T(8,128)(2,1)S(1)} %bitcast.98, bf16[768,256]{1,0:T(8,128)(2,1)S(1)} %bitcast.99, bf16[768,256]{1,0:T(8,128)(2,1)S(1)} %bitcast.96), kind=kOutput, calls=%fused_computation | convolution fusion | flops 3229614080 | bytes 13107200 | tf_op jit(solution)/shard_map/crk,rw->ckw/dot_general | solution.py:362
  (26 shorter events, 0.4 us)
Async XLA Ops:
  0.7 1.0 copy-start.2
  37.0 1.7 copy-start
  37.0 3.3 %copy-start.3 = (bf16[2048,1024]{1,0:T(8,128)(2,1)S(1)}, bf16[2048,1024]{1,0:T(8,128)(2,1)}, u32[]{:S(2)}) copy-start(bf16[2048,1024]{1,0:T(8,128)(2,1)} %param.3) | copy-start | bytes 12582916
  150.1 34.0 %copy-start.1 = (bf16[2,4,4,48,1024]{4,3,2,1,0:T(8,128)(2,1)S(1)}, bf16[2,4,4,48,1024]{4,3,2,1,0:T(8,128)(2,1)}, u32[]{:S(2)}) copy-start(bf16[2,4,4,48,1024]{4,3,2,1,0:T(8,128)(2,1)} %copy-done) | copy-start | bytes 9437188
